TPU v7x, 32 devices: a whole 2x2x4 slice. The times are simulated.
32 devices in a mesh: req: 8 (over z, x), head: 4 (over y, core).
Axes of the slice: x: 2, y: 2, z: 4, core: 2. Of those that a mesh axis runs over, the one named last changes fastest.
Arguments:
- resid: bfloat16 [32, 4, 2048], P('req'), may hold values from -6 to 6
- proj: bfloat16 [32, 4, 3, 2048], P('req', None, None, 'head'), may hold values from -6 to 6
- conv_cache: bfloat16 [32, 3, 3, 2048], P('req', None, None, 'head'), may hold values from -6 to 6
- conv_weight: bfloat16 [4, 3, 2048], P(None, None, 'head'), may hold values from -3 to 3
- forget_bias: float32 [2048], P('head'), may hold values from -2 to 6
- owner: int32 [32], replicated, may hold values from 0 to 31, each once
- lengths: int32 [32], replicated, may hold values from 0 to 4096, as said below
- old_state: bfloat16 [32, 16, 128, 128], P('req', 'head'), may hold values from -6 to 6
- norm_gain: float32 [2048], P('head'), may hold values from 0.5 to 1.5
- out_weight: bfloat16 [2048, 2048], P('head'), may hold values from -0.125 to 0.125
Outputs:
- mixed: bfloat16 [32, 4, 2048], P('req')
- new_state: bfloat16 [32, 16, 128, 128], P('req', 'head')
Inputs may be any that keep to these rules, and one draw needn't show every extreme that they name: `lengths`: short requests (below 3) and long ones are mixed; some request has length 0 and some 4096.
All inputs are finite; a program needn't handle non-finite values.
Results may differ from a plain program's by a relative error of at most 0.015.
Values may be sent and summed in bfloat16 or wider, within the bound.
No kernel may reach another device: no remote copies, remote signals or barrier semaphores. Data moves between devices by JAX's collectives and lax.ppermute only.
A program may use at most 64 MiB of HBM per device.

v0:
```python
import jax
import jax.numpy as jnp
from jax import lax
from jax.sharding import PartitionSpec as P


def convolve(proj, conv_cache, conv_weight, lens):
    taps = conv_weight.shape[0]
    new_tokens = proj.shape[1]
    joined = jnp.concatenate([conv_cache, proj], axis=1).astype(jnp.float32)
    places = lens[:, None] + jnp.arange(-(taps - 1), new_tokens, dtype=jnp.int32)[None, :]
    joined = jnp.where((places >= 0)[:, :, None, None], joined, jnp.float32(0.0))
    summed = jnp.zeros(proj.shape, jnp.float32)
    for offset in range(taps):
        begin_at = taps - 1 - offset
        summed = summed + joined[:, begin_at : begin_at + new_tokens] * conv_weight[offset].astype(
            jnp.float32
        )
    return jax.nn.silu(summed).astype(jnp.bfloat16)


def recurrence(convolved, relocated, lens, forget_bias, norm_gain, head_size):
    local_reqs, new_tokens, _, channels = convolved.shape
    head_count = channels // head_size
    values = convolved.astype(jnp.float32).reshape(local_reqs, new_tokens, 3, head_count, head_size)
    queries = values[:, :, 0]
    keep_rate = jax.nn.sigmoid(values[:, :, 1] + forget_bias.reshape(head_count, head_size))
    inputs = values[:, :, 2]
    current = relocated.astype(jnp.float32) * (lens > 0).astype(jnp.float32)[:, None, None, None]
    outputs = []
    for position in range(new_tokens):
        rate_now = keep_rate[:, position]
        current = (
            rate_now[..., None] * current
            + (1.0 - rate_now)[..., None] * inputs[:, position][:, :, None, :]
        )
        outputs.append(jnp.einsum("rhk,rhkv->rhv", queries[:, position], current))
    stacked = jnp.stack(outputs, axis=1)
    inverse_rms = lax.rsqrt(jnp.mean(stacked * stacked, axis=-1, keepdims=True) + 1e-06)
    normed = (stacked * inverse_rms).reshape(local_reqs, new_tokens, channels) * norm_gain
    return (normed.astype(jnp.bfloat16), current.astype(jnp.bfloat16))


def body(
    resid,
    proj,
    conv_cache,
    conv_weight,
    forget_bias,
    owner,
    lengths,
    old_state,
    norm_gain,
    out_weight,
):
    local_reqs = resid.shape[0]
    new_tokens = resid.shape[1]
    devices = lax.axis_size("req")
    own_index = lax.axis_index("req")
    total_reqs = owner.shape[0]
    head_size = old_state.shape[-1]
    inverse = (
        jnp.zeros((total_reqs,), jnp.int32).at[owner].set(jnp.arange(total_reqs, dtype=jnp.int32))
    )
    local_lens = lax.dynamic_slice_in_dim(lengths, own_index * local_reqs, local_reqs)
    convolved = convolve(proj, conv_cache, conv_weight, local_lens)
    pieces = old_state.reshape(local_reqs, devices, -1)
    spread = lax.all_to_all(pieces, "req", split_axis=1, concat_axis=0, tiled=True).reshape(
        total_reqs, -1
    )
    picked = jnp.take(spread, inverse, axis=0).reshape(devices, local_reqs, 1, -1)
    routed = lax.all_to_all(picked, "req", split_axis=0, concat_axis=2, tiled=True)
    relocated = routed.reshape(old_state.shape)
    normed, new_state = recurrence(
        convolved, relocated, local_lens, forget_bias, norm_gain, head_size
    )
    flat_normed = normed.reshape(local_reqs * new_tokens, -1)
    flat_resid = resid.reshape(local_reqs * new_tokens, -1)
    partial_value = jnp.dot(flat_normed, out_weight, preferred_element_type=jnp.float32)
    summed = lax.psum(partial_value, "head")
    mixed = (flat_resid.astype(jnp.float32) + summed).astype(jnp.bfloat16).reshape(resid.shape)
    return (mixed, new_state)


def solution(mesh):
    in_specs = (
        P("req", None, None),
        P("req", None, None, "head"),
        P("req", None, None, "head"),
        P(None, None, "head"),
        P("head"),
        P(),
        P(),
        P("req", "head", None, None),
        P("head"),
        P("head", None),
    )
    out_specs = (P("req", None, None), P("req", "head", None, None))
    return jax.shard_map(body, mesh=mesh, in_specs=in_specs, out_specs=out_specs, check_vma=False)
```

profile of v0, /device:TPU:0, one launch (start us, length us, event | category | flops | bytes accessed | tf_op | source)
XLA Modules:
  0.0 103.1 jit_solution(8104832526261652992)
XLA Ops:
  7.2 0.0 copy-start
  7.2 0.0 copy-start.4
  7.2 0.0 copy-start.3
  7.2 0.0 copy-start.7
  7.2 0.0 copy-start.2
  7.2 0.0 copy-start.8
  7.2 0.0 copy-start.5
  7.2 1.4 %reshape.167 = bf16[4,8,8192]{2,1,0:T(8,128)(2,1)S(1)} reshape(bf16[4,4,128,128]{3,2,1,0:T(8,128)(2,1)} %param.17) | data formatting | bytes 1048576 | tf_op jit(solution)/shard_map/reshape | solution.py:67
  8.6 1.2 %copy.27 = bf16[4,8,8192]{2,0,1:T(4,128)(2,1)} copy(bf16[4,8,8192]{2,1,0:T(8,128)(2,1)S(1)} %reshape.167) | data formatting | bytes 1048576 | tf_op jit(solution)/shard_map/reshape | solution.py:67
  9.8 7.3 %all-to-all-start = ((bf16[4,8,8192]{2,0,1:T(4,128)(2,1)}), bf16[4,8,8192]{2,0,1:T(4,128)(2,1)S(1)}, u32[]{:S(2)}, u32[]{:S(2)}) async-start(bf16[4,8,8192]{2,0,1:T(4,128)(2,1)} %copy.27), calls=%async_computation | async-start | bytes 1048576 | tf_op jit(solution)/shard_map/all_to_all | solution.py:68
  17.1 0.0 copy-done.4
  17.1 0.0 copy-done.3
  17.2 0.0 copy-done.7
  17.2 0.1 compare_convert_fusion
  17.3 0.1 add_compare_fusion
  17.4 0.0 copy-done.2
  17.4 0.1 convert_select_fusion
  17.5 0.1 fusion.21
  17.6 0.0 copy-done.8
  17.7 0.7 scatter_custom_fusion
  18.4 0.1 broadcast_in_dim.46
  18.5 0.0 copy-done.5
  18.6 13.0 %all-to-all-done = bf16[4,8,8192]{2,0,1:T(4,128)(2,1)S(1)} async-done(((bf16[4,8,8192]{2,0,1:T(4,128)(2,1)}), bf16[4,8,8192]{2,0,1:T(4,128)(2,1)S(1)}, u32[]{:S(2)}, u32[]{:S(2)}) %all-to-all-start) | async-done | bytes 524320 | tf_op jit(solution)/shard_map/all_to_all | solution.py:68
  31.6 0.1 reshape.168
  31.7 0.9 gather_fusion
  32.6 0.0 copy-start.1
  32.6 0.2 gather.7
  32.8 1.1 %bitcast_select_fusion = bf16[8,4,1,8192]{3,1,2,0:T(4,128)(2,1)} fusion(bf16[8,4,1,8192]{3,1,0,2:T(4,128)(2,1)S(1)} %gather.7, pred[8,4]{1,0:T(8,128)(4,1)S(1)} %broadcast_in_dim.46), kind=kLoop, calls=%fused_computation.11 | loop fusion | flops 262144 | bytes 1048608 | tf_op jit(solution)/shard_map/jit(_take)/select_n | solution.py:71
  33.9 3.6 %all-to-all-start.1 = ((bf16[8,4,1,8192]{3,1,2,0:T(4,128)(2,1)}), bf16[8,4,1,8192]{3,1,2,0:T(4,128)(2,1)S(1)}, u32[]{:S(2)}, u32[]{:S(2)}) async-start(bf16[8,4,1,8192]{3,1,2,0:T(4,128)(2,1)} %bitcast_select_fusion), calls=%async_computation.1 | async-start | bytes 1048576 | tf_op jit(solution)/shard_map/all_to_all | solution.py:72
  37.5 0.0 all-reduce.2.cloned.1.call-start
  37.6 0.0 copy-done.1
  37.7 14.5 %all-to-all-done.1 = bf16[8,4,1,8192]{3,1,2,0:T(4,128)(2,1)S(1)} async-done(((bf16[8,4,1,8192]{3,1,2,0:T(4,128)(2,1)}), bf16[8,4,1,8192]{3,1,2,0:T(4,128)(2,1)S(1)}, u32[]{:S(2)}, u32[]{:S(2)}) %all-to-all-start.1) | async-done | bytes 524320 | tf_op jit(solution)/shard_map/all_to_all | solution.py:72
  52.2 0.1 convert_bitcast_fusion
  52.3 1.6 %copy.29 = f32[1,4,8,1,8192]{4,2,1,3,0:T(8,128)} copy(f32[1,4,8,1,8192]{4,1,2,3,0:T(4,128)S(1)} %convert_bitcast_fusion) | data formatting | bytes 2097152 | tf_op jit(solution)/shard_map/convert_element_type | solution.py:29
  53.9 1.4 %reshape.175 = f32[4,4,128,128]{3,2,1,0:T(8,128)S(1)} reshape(f32[1,4,8,1,8192]{4,2,1,3,0:T(8,128)} %copy.29) | data formatting | bytes 2097152 | tf_op jit(solution)/shard_map/convert_element_type | solution.py:29
  55.2 0.7 fusion.3
  56.0 1.5 %fusion = f32[4,4,1,128]{3,2,1,0:T(1,128)S(1)} fusion(f32[4,4,128,128]{3,2,1,0:T(8,128)S(1)} %reshape.175, f32[4,4,128]{2,1,0:T(4,128)S(1)} %get-tuple-element.15, f32[4,4,128]{2,1,0:T(4,128)S(1)} %get-tuple-element.11, f32[4,4,128]{2,1,0:T(4,128)S(1)} %get-tuple-element.7, f32[4,4,128]{2,1,0:T(4,128)S(1)} %get-tuple-element.12, ...), kind=kOutput, calls=%fused_computation.7 | convolution fusion | flops 2359296 | bytes 1110032 | tf_op jit(solution)/shard_map/rhk,rhkv->rhv/dot_general | solution.py:37
  57.4 2.4 %fusion.34 = f32[4,4,1,128]{3,2,1,0:T(1,128)S(1)} fusion(bf16[4,4,128,1]{2,1,0,3:T(4,128)(2,1)S(1)} %get-tuple-element.18, f32[4,4,128,128]{3,2,1,0:T(8,128)S(1)} %reshape.175, f32[4,4,128]{2,1,0:T(4,128)S(1)} %get-tuple-element.14, f32[4,4,128]{2,1,0:T(4,128)S(1)} %get-tuple-element.10, f32[4,4,128]{2,1,0:T(4,128)S(1)} %get-tuple-element.6, ...), kind=kOutput, calls=%fused_computation.67 | convolution fusion | flops 3145728 | bytes 1134608 | tf_op jit(solution)/shard_map/rhk,rhkv->rhv/dot_general | solution.py:37
  59.8 0.0 copy-start.6
  59.8 2.9 %fusion.2 = f32[4,4,1,128]{3,2,1,0:T(1,128)S(1)} fusion(f32[4,4,128]{2,1,0:T(4,128)S(1)} %get-tuple-element.13, f32[4,4,128]{2,1,0:T(4,128)S(1)} %get-tuple-element.9, f32[4,4,128]{2,1,0:T(4,128)S(1)} %get-tuple-element.5, bf16[4,4,128,1]{2,1,0,3:T(4,128)(2,1)S(1)} %get-tuple-element.17, f32[4,4,128,128]{3,2,1,0:T(8,128)S(1)} %reshape.175, ...), kind=kOutput, calls=%fused_computation.9 | convolution fusion | flops 3932160 | bytes 1159184 | tf_op jit(solution)/shard_map/rhk,rhkv->rhv/dot_general | solution.py:37
  62.7 0.1 fusion.29
  62.9 0.1 mul.212
  63.0 0.0 copy-done
  63.0 0.0 copy-done.6
  63.0 1.0 %fusion.30 = f32[16,2048]{1,0:T(8,128)} fusion(bf16[512,2048]{1,0:T(8,128)(2,1)S(1)} %copy-done, f32[16,512]{1,0:T(8,128)S(1)} %stack.32, f32[2,8,4,128]{3,2,1,0:T(4,128)S(1)} %bitcast.112, f32[512]{0:T(512)S(1)} %copy-done.6), kind=kOutput, calls=%fused_computation.51 | convolution fusion | flops 33579008 | bytes 2295808 | tf_op jit(solution)/shard_map/dot_general | solution.py:79
  64.0 0.0 all-reduce.2.cloned.1.call-update
  64.1 3.2 %fusion.1 = bf16[4,4,128,128]{3,2,1,0:T(8,128)(2,1)} fusion(f32[4,4,128]{2,1,0:T(4,128)S(1)} %get-tuple-element.13, f32[4,4,128]{2,1,0:T(4,128)S(1)} %get-tuple-element.9, f32[4,4,128]{2,1,0:T(4,128)S(1)} %get-tuple-element.5, f32[4,4,128]{2,1,0:T(4,128)S(1)} %get-tuple-element.14, f32[4,4,128]{2,1,0:T(4,128)S(1)} %get-tuple-element.10, ...), kind=kLoop, calls=%fused_computation.8 | loop fusion | flops 3670016 | bytes 1671184 | tf_op jit(solution)/shard_map/convert_element_type | solution.py:41
  67.3 27.5 %all-reduce.2.cloned.1.call-done = f32[16,2048]{1,0:T(8,128)} async-done(((f32[16,2048]{1,0:T(8,128)}), f32[16,2048]{1,0:T(8,128)}) %all-reduce.2.cloned.1.call-update) | async-done | bytes 131088 | tf_op jit(solution)/shard_map/psum | solution.py:80
  94.7 0.9 add_convert_fusion
  95.6 0.7 reshape.169
  (24 shorter events, 0.3 us)
Async XLA Ops:
  7.2 55.8 %copy-start = (bf16[512,2048]{1,0:T(8,128)(2,1)S(1)}, bf16[512,2048]{1,0:T(8,128)(2,1)}, u32[]{:S(2)}) copy-start(bf16[512,2048]{1,0:T(8,128)(2,1)} %param.19) | copy-start | bytes 6291460
  7.2 9.9 %copy-start.4 = (bf16[4,3,3,512]{3,0,2,1:T(4,128)(2,1)S(1)}, bf16[4,3,3,512]{3,0,2,1:T(4,128)(2,1)}, u32[]{:S(2)}) copy-start(bf16[4,3,3,512]{3,0,2,1:T(4,128)(2,1)} %param.12) | copy-start | bytes 110596
  7.2 10.0 %copy-start.3 = (bf16[4,3,512]{2,0,1:T(4,128)(2,1)S(1)}, bf16[4,3,512]{2,0,1:T(4,128)(2,1)}, u32[]{:S(2)}) copy-start(bf16[4,3,512]{2,0,1:T(4,128)(2,1)} %param.13) | copy-start | bytes 36868
  7.2 10.0 %copy-start.7 = (s32[32]{0:T(128)S(1)}, s32[32]{0:T(128)}, u32[]{:S(2)}) copy-start(s32[32]{0:T(128)} %param.16) | copy-start | bytes 388
  7.2 10.2 %copy-start.2 = (bf16[4,4,3,512]{3,1,2,0:T(4,128)(2,1)S(1)}, bf16[4,4,3,512]{3,1,2,0:T(4,128)(2,1)}, u32[]{:S(2)}) copy-start(bf16[4,4,3,512]{3,1,2,0:T(4,128)(2,1)} %param.11) | copy-start | bytes 147460
  7.2 10.4 %copy-start.8 = (s32[32]{0:T(128)S(1)}, s32[32]{0:T(128)}, u32[]{:S(2)}) copy-start(s32[32]{0:T(128)} %param.15) | copy-start | bytes 388
  7.2 11.3 %copy-start.5 = (f32[512]{0:T(512)S(1)}, f32[512]{0:T(512)}, u32[]{:S(2)}) copy-start(f32[512]{0:T(512)} %param.14) | copy-start | bytes 6148
  9.8 21.7 %all-to-all-start = ((bf16[4,8,8192]{2,0,1:T(4,128)(2,1)}), bf16[4,8,8192]{2,0,1:T(4,128)(2,1)S(1)}, u32[]{:S(2)}, u32[]{:S(2)}) async-start(bf16[4,8,8192]{2,0,1:T(4,128)(2,1)} %copy.27), calls=%async_computation | async-start | bytes 1048576 | tf_op jit(solution)/shard_map/all_to_all | solution.py:68
  32.6 5.0 %copy-start.1 = (bf16[4,4,2048]{2,1,0:T(4,128)(2,1)S(1)}, bf16[4,4,2048]{2,1,0:T(4,128)(2,1)}, u32[]{:S(2)}) copy-start(bf16[4,4,2048]{2,1,0:T(4,128)(2,1)} %param.10) | copy-start | bytes 196612
  33.9 18.3 %all-to-all-start.1 = ((bf16[8,4,1,8192]{3,1,2,0:T(4,128)(2,1)}), bf16[8,4,1,8192]{3,1,2,0:T(4,128)(2,1)S(1)}, u32[]{:S(2)}, u32[]{:S(2)}) async-start(bf16[8,4,1,8192]{3,1,2,0:T(4,128)(2,1)} %bitcast_select_fusion), calls=%async_computation.1 | async-start | bytes 1048576 | tf_op jit(solution)/shard_map/all_to_all | solution.py:72
  37.5 57.2 %all-reduce.2.cloned.1.call-start = ((), (), s32[]{:S(2)}) async-start(), calls=%async_computation.2 | async-start | bytes 262144 | tf_op jit(solution)/shard_map/psum | solution.py:80
  59.8 3.2 %copy-start.6 = (f32[512]{0:T(512)S(1)}, f32[512]{0:T(512)}, u32[]{:S(2)}) copy-start(f32[512]{0:T(512)} %param.18) | copy-start | bytes 6148
Sparse Core Ops, SparseCore 0:
  64.2 30.4 all-reduce.1
where the time goes:
time: 103 us
  waiting for transfers between devices  55 us (53%)
  between operations  14.4 us (14%)
  starting transfers between devices  10.9 us (11%)
  matrix products  8.49 us (8%)
  local copies, waits for them, and re-layouts  8.43 us (8%)
  other arithmetic  5.91 us (6%)
    psum x1, waiting for transfers between devices, body(): summed = lax.psum(partial_value, 'head')  27.5 us
    all_to_all x1, waiting for transfers between devices, body(): lax.all_to_all(picked, 'req', split_axis=0, concat_axis=2, tiled=True)  14.5 us
    all_to_all x1, waiting for transfers between devices, body(): lax.all_to_all(pieces, 'req', split_axis=1, concat_axis=0, tiled=True)  13 us
    dot_general x4, matrix products, recurrence(): outputs.append(jnp.einsum('rhk,rhkv->rhv', queries[:, position], current))  7.46 us
    all_to_all x1, starting transfers between devices, body(): lax.all_to_all(pieces, 'req', split_axis=1, concat_axis=0, tiled=True)  7.25 us
    all_to_all x1, starting transfers between devices, body(): lax.all_to_all(picked, 'req', split_axis=0, concat_axis=2, tiled=True)  3.64 us
    convert_element_type x1, other arithmetic, recurrence(): return (normed.astype(jnp.bfloat16), current.astype(jnp.bfloat16))  3.19 us
    convert_element_type x2, local copies, waits for them, and re-layouts, recurrence(): relocated.astype(jnp.float32)  2.97 us
  transfers between devices with their start and end apart: 3, of which 3 were waited for; matrix products, arithmetic and copies ran while one was open for 4% of the time, Pallas kernels for 0%

commit v1 on v0

--- a/solution.py
+++ b/solution.py
@@ -77,7 +77,7 @@
     flat_normed = normed.reshape(local_reqs * new_tokens, -1)
     flat_resid = resid.reshape(local_reqs * new_tokens, -1)
     partial_value = jnp.dot(flat_normed, out_weight, preferred_element_type=jnp.float32)
-    summed = lax.psum(partial_value, "head")
+    summed = jnp.sum(lax.all_gather(partial_value, "head"), axis=0)
     mixed = (flat_resid.astype(jnp.float32) + summed).astype(jnp.bfloat16).reshape(resid.shape)
     return (mixed, new_state)
 

time: 103 us -> 68.3 us (0.66)
  waiting for transfers between devices: 55 us -> 27.6 us
  between operations: 14.4 us -> 0.98 us
  blocking collectives: 0 us -> 7.19 us
    psum x1 -> x0, waiting for transfers between devices: 27.5 us -> none  [body(): summed = lax.psum(partial_value, 'head')]
    all_gather x0 -> x1, blocking collectives: none -> 7.19 us  [body(): summed = jnp.sum(lax.all_gather(partial_value, 'head'), axis=0)]
  transfers between devices with their start and end apart: 3 -> 2, of which waited for: 3 -> 2; matrix products, arithmetic and copies ran while one was open for 4% -> 2% of each run, Pallas kernels for 0% -> 0%
where the time goes in v1:
time: 68.3 us; the launch traced here: 68 us
  waiting for transfers between devices  27.6 us (40%)
  starting transfers between devices  10.9 us (16%)
  matrix products  7.84 us (11%)
  local copies, waits for them, and re-layouts  7.78 us (11%)
  blocking collectives  7.19 us (11%)
  other arithmetic  5.67 us (8%)
  between operations  0.98 us (1%)
    all_to_all x1, waiting for transfers between devices, body(): lax.all_to_all(picked, 'req', split_axis=0, concat_axis=2, tiled=True)  14.6 us
    all_to_all x1, waiting for transfers between devices, body(): lax.all_to_all(pieces, 'req', split_axis=1, concat_axis=0, tiled=True)  13 us
    dot_general x4, matrix products, recurrence(): outputs.append(jnp.einsum('rhk,rhkv->rhv', queries[:, position], current))  7.46 us
    all_to_all x1, starting transfers between devices, body(): lax.all_to_all(pieces, 'req', split_axis=1, concat_axis=0, tiled=True)  7.25 us
    all_gather x1, blocking collectives, body(): summed = jnp.sum(lax.all_gather(partial_value, 'head'), axis=0)  7.19 us
    all_to_all x1, starting transfers between devices, body(): lax.all_to_all(picked, 'req', split_axis=0, concat_axis=2, tiled=True)  3.64 us
    convert_element_type x1, other arithmetic, recurrence(): return (normed.astype(jnp.bfloat16), current.astype(jnp.bfloat16))  3.19 us
    convert_element_type x2, local copies, waits for them, and re-layouts, recurrence(): relocated.astype(jnp.float32)  2.97 us
  transfers between devices with their start and end apart: 2, of which 2 were waited for; matrix products, arithmetic and copies ran while one was open for 2% of the time, Pallas kernels for 0%

profile of v1, /device:TPU:0, one launch (start us, length us, event | category | flops | bytes accessed | tf_op | source)
XLA Modules:
  0.0 68.0 jit_solution(1179416869927369285)
XLA Ops:
  0.6 0.0 copy-start
  0.6 0.0 copy-start.8
  0.7 0.0 copy-start.3
  0.7 0.0 copy-start.4
  0.7 0.0 copy-start.7
  0.7 0.0 copy-start.2
  0.7 0.0 copy-start.5
  0.7 1.4 %reshape.164 = bf16[4,8,8192]{2,1,0:T(8,128)(2,1)S(1)} reshape(bf16[4,4,128,128]{3,2,1,0:T(8,128)(2,1)} %param.17) | data formatting | bytes 1048576 | tf_op jit(solution)/shard_map/reshape | solution.py:67
  2.1 1.2 %copy.27 = bf16[4,8,8192]{2,0,1:T(4,128)(2,1)} copy(bf16[4,8,8192]{2,1,0:T(8,128)(2,1)S(1)} %reshape.164) | data formatting | bytes 1048576 | tf_op jit(solution)/shard_map/reshape | solution.py:67
  3.3 7.3 %all-to-all-start = ((bf16[4,8,8192]{2,0,1:T(4,128)(2,1)}), bf16[4,8,8192]{2,0,1:T(4,128)(2,1)S(1)}, u32[]{:S(2)}, u32[]{:S(2)}) async-start(bf16[4,8,8192]{2,0,1:T(4,128)(2,1)} %copy.27), calls=%async_computation | async-start | bytes 1048576 | tf_op jit(solution)/shard_map/all_to_all | solution.py:68
  10.6 0.0 copy-done.8
  10.6 0.7 scatter_custom_fusion
  11.3 0.1 broadcast_in_dim.46
  11.4 0.0 copy-done.3
  11.4 0.0 copy-done.4
  11.5 0.0 copy-done.7
  11.5 0.1 compare_convert_fusion
  11.6 0.1 add_compare_fusion
  11.6 0.0 copy-done.2
  11.7 0.1 convert_select_fusion
  11.7 0.1 fusion.21
  12.0 0.0 copy-done.5
  12.0 13.0 %all-to-all-done = bf16[4,8,8192]{2,0,1:T(4,128)(2,1)S(1)} async-done(((bf16[4,8,8192]{2,0,1:T(4,128)(2,1)}), bf16[4,8,8192]{2,0,1:T(4,128)(2,1)S(1)}, u32[]{:S(2)}, u32[]{:S(2)}) %all-to-all-start) | async-done | bytes 524320 | tf_op jit(solution)/shard_map/all_to_all | solution.py:68
  25.1 0.1 reshape.165
  25.2 0.9 %gather_fusion = bf16[32,8192]{1,0:T(8,128)(2,1)S(1)} fusion(bf16[32,8192]{1,0:T(8,128)(2,1)S(1)} %reshape.165, s32[1024]{0:T(1024)S(1)} %pad_clamp_fusion), kind=kCustom, calls=%fused_computation | custom fusion | bytes 1048704 | tf_op jit(solution)/shard_map/jit(_take)/gather | solution.py:71
  26.1 0.2 gather.7
  26.3 1.1 %bitcast_select_fusion = bf16[8,4,1,8192]{3,1,2,0:T(4,128)(2,1)} fusion(bf16[8,4,1,8192]{3,1,0,2:T(4,128)(2,1)S(1)} %gather.7, pred[8,4]{1,0:T(8,128)(4,1)S(1)} %broadcast_in_dim.46), kind=kLoop, calls=%fused_computation.11 | loop fusion | flops 262144 | bytes 1048608 | tf_op jit(solution)/shard_map/jit(_take)/select_n | solution.py:71
  27.4 3.6 %all-to-all-start.1 = ((bf16[8,4,1,8192]{3,1,2,0:T(4,128)(2,1)}), bf16[8,4,1,8192]{3,1,2,0:T(4,128)(2,1)S(1)}, u32[]{:S(2)}, u32[]{:S(2)}) async-start(bf16[8,4,1,8192]{3,1,2,0:T(4,128)(2,1)} %bitcast_select_fusion), calls=%async_computation.1 | async-start | bytes 1048576 | tf_op jit(solution)/shard_map/all_to_all | solution.py:72
  31.1 14.6 %all-to-all-done.1 = bf16[8,4,1,8192]{3,1,2,0:T(4,128)(2,1)S(1)} async-done(((bf16[8,4,1,8192]{3,1,2,0:T(4,128)(2,1)}), bf16[8,4,1,8192]{3,1,2,0:T(4,128)(2,1)S(1)}, u32[]{:S(2)}, u32[]{:S(2)}) %all-to-all-start.1) | async-done | bytes 524320 | tf_op jit(solution)/shard_map/all_to_all | solution.py:72
  45.7 0.1 convert_bitcast_fusion
  45.7 1.6 %copy.29 = f32[1,4,8,1,8192]{4,2,1,3,0:T(8,128)} copy(f32[1,4,8,1,8192]{4,1,2,3,0:T(4,128)S(1)} %convert_bitcast_fusion) | data formatting | bytes 2097152 | tf_op jit(solution)/shard_map/convert_element_type | solution.py:29
  47.3 1.4 %reshape.170 = f32[4,4,128,128]{3,2,1,0:T(8,128)S(1)} reshape(f32[1,4,8,1,8192]{4,2,1,3,0:T(8,128)} %copy.29) | data formatting | bytes 2097152 | tf_op jit(solution)/shard_map/convert_element_type | solution.py:29
  48.7 3.2 %fusion.1 = bf16[4,4,128,128]{3,2,1,0:T(8,128)(2,1)} fusion(f32[4,4,128]{2,1,0:T(4,128)S(1)} %get-tuple-element.13, f32[4,4,128]{2,1,0:T(4,128)S(1)} %get-tuple-element.9, f32[4,4,128]{2,1,0:T(4,128)S(1)} %get-tuple-element.5, f32[4,4,128]{2,1,0:T(4,128)S(1)} %get-tuple-element.14, f32[4,4,128]{2,1,0:T(4,128)S(1)} %get-tuple-element.10, ...), kind=kLoop, calls=%fused_computation.8 | loop fusion | flops 3670016 | bytes 1671184 | tf_op jit(solution)/shard_map/convert_element_type | solution.py:41
  51.9 2.9 %fusion.2 = f32[4,4,1,128]{3,2,1,0:T(1,128)S(1)} fusion(f32[4,4,128]{2,1,0:T(4,128)S(1)} %get-tuple-element.13, f32[4,4,128]{2,1,0:T(4,128)S(1)} %get-tuple-element.9, f32[4,4,128]{2,1,0:T(4,128)S(1)} %get-tuple-element.5, bf16[4,4,128,1]{2,1,0,3:T(4,128)(2,1)S(1)} %get-tuple-element.17, f32[4,4,128,128]{3,2,1,0:T(8,128)S(1)} %reshape.170, ...), kind=kOutput, calls=%fused_computation.9 | convolution fusion | flops 3932160 | bytes 1159184 | tf_op jit(solution)/shard_map/rhk,rhkv->rhv/dot_general | solution.py:37
  54.8 1.5 %fusion = f32[4,4,1,128]{3,2,1,0:T(1,128)S(1)} fusion(f32[4,4,128,128]{3,2,1,0:T(8,128)S(1)} %reshape.170, f32[4,4,128]{2,1,0:T(4,128)S(1)} %get-tuple-element.15, f32[4,4,128]{2,1,0:T(4,128)S(1)} %get-tuple-element.11, f32[4,4,128]{2,1,0:T(4,128)S(1)} %get-tuple-element.7, f32[4,4,128]{2,1,0:T(4,128)S(1)} %get-tuple-element.12, ...), kind=kOutput, calls=%fused_computation.7 | convolution fusion | flops 2359296 | bytes 1110032 | tf_op jit(solution)/shard_map/rhk,rhkv->rhv/dot_general | solution.py:37
  56.2 0.0 copy-start.6
  56.3 2.4 %fusion.34 = f32[4,4,1,128]{3,2,1,0:T(1,128)S(1)} fusion(bf16[4,4,128,1]{2,1,0,3:T(4,128)(2,1)S(1)} %get-tuple-element.18, f32[4,4,128,128]{3,2,1,0:T(8,128)S(1)} %reshape.170, f32[4,4,128]{2,1,0:T(4,128)S(1)} %get-tuple-element.14, f32[4,4,128]{2,1,0:T(4,128)S(1)} %get-tuple-element.10, f32[4,4,128]{2,1,0:T(4,128)S(1)} %get-tuple-element.6, ...), kind=kOutput, calls=%fused_computation.67 | convolution fusion | flops 3145728 | bytes 1134608 | tf_op jit(solution)/shard_map/rhk,rhkv->rhv/dot_general | solution.py:37
  58.6 0.7 %fusion.3 = f32[4,4,1,128]{3,2,1,0:T(1,128)S(1)} fusion(f32[4,4,128,128]{3,2,1,0:T(8,128)S(1)} %reshape.170, f32[4,4,128]{2,1,0:T(4,128)S(1)} %get-tuple-element.12, f32[4,4,128]{2,1,0:T(4,128)S(1)} %get-tuple-element.8, f32[4]{0:T(128)S(1)} %get-tuple-element.2, f32[4,4,128]{2,1,0:T(4,128)S(1)} %get-tuple-element.4, ...), kind=kOutput, calls=%fused_computation.10 | convolution fusion | flops 1572864 | bytes 1085456 | tf_op jit(solution)/shard_map/rhk,rhkv->rhv/dot_general | solution.py:37
  59.4 0.0 copy-start.1
  59.4 0.1 fusion.29
  59.6 0.1 mul.212
  59.6 0.0 copy-done
  59.6 0.0 copy-done.6
  59.7 0.4 fusion.30
  60.0 7.2 %all-gather = f32[64,2048]{1,0:T(8,128)S(1)} all-gather(f32[16,2048]{1,0:T(8,128)S(1)} %fusion.30), channel_id=2, replica_groups=mesh['req'=8,'head'=4] {'head'}, dimensions={0}, use_global_device_ids=true | all-gather | bytes 655360 | tf_op jit(solution)/shard_map/all_gather | solution.py:80
  67.3 0.0 copy-done.1
  67.3 0.7 add_convert_fusion
  (25 shorter events, 0.3 us)
Async XLA Ops:
  0.6 59.0 %copy-start = (bf16[512,2048]{1,0:T(8,128)(2,1)S(1)}, bf16[512,2048]{1,0:T(8,128)(2,1)}, u32[]{:S(2)}) copy-start(bf16[512,2048]{1,0:T(8,128)(2,1)} %param.19) | copy-start | bytes 6291460
  0.6 9.9 %copy-start.8 = (s32[32]{0:T(128)S(1)}, s32[32]{0:T(128)}, u32[]{:S(2)}) copy-start(s32[32]{0:T(128)} %param.15) | copy-start | bytes 388
  0.7 10.7 %copy-start.3 = (bf16[4,3,512]{2,0,1:T(4,128)(2,1)S(1)}, bf16[4,3,512]{2,0,1:T(4,128)(2,1)}, u32[]{:S(2)}) copy-start(bf16[4,3,512]{2,0,1:T(4,128)(2,1)} %param.13) | copy-start | bytes 36868
  0.7 10.8 %copy-start.4 = (bf16[4,3,3,512]{3,0,2,1:T(4,128)(2,1)S(1)}, bf16[4,3,3,512]{3,0,2,1:T(4,128)(2,1)}, u32[]{:S(2)}) copy-start(bf16[4,3,3,512]{3,0,2,1:T(4,128)(2,1)} %param.12) | copy-start | bytes 110596
  0.7 10.8 %copy-start.7 = (s32[32]{0:T(128)S(1)}, s32[32]{0:T(128)}, u32[]{:S(2)}) copy-start(s32[32]{0:T(128)} %param.16) | copy-start | bytes 388
  0.7 11.0 %copy-start.2 = (bf16[4,4,3,512]{3,1,2,0:T(4,128)(2,1)S(1)}, bf16[4,4,3,512]{3,1,2,0:T(4,128)(2,1)}, u32[]{:S(2)}) copy-start(bf16[4,4,3,512]{3,1,2,0:T(4,128)(2,1)} %param.11) | copy-start | bytes 147460
  0.7 11.3 %copy-start.5 = (f32[512]{0:T(512)S(1)}, f32[512]{0:T(512)}, u32[]{:S(2)}) copy-start(f32[512]{0:T(512)} %param.14) | copy-start | bytes 6148
  3.3 21.7 %all-to-all-start = ((bf16[4,8,8192]{2,0,1:T(4,128)(2,1)}), bf16[4,8,8192]{2,0,1:T(4,128)(2,1)S(1)}, u32[]{:S(2)}, u32[]{:S(2)}) async-start(bf16[4,8,8192]{2,0,1:T(4,128)(2,1)} %copy.27), calls=%async_computation | async-start | bytes 1048576 | tf_op jit(solution)/shard_map/all_to_all | solution.py:68
  27.4 18.3 %all-to-all-start.1 = ((bf16[8,4,1,8192]{3,1,2,0:T(4,128)(2,1)}), bf16[8,4,1,8192]{3,1,2,0:T(4,128)(2,1)S(1)}, u32[]{:S(2)}, u32[]{:S(2)}) async-start(bf16[8,4,1,8192]{3,1,2,0:T(4,128)(2,1)} %bitcast_select_fusion), calls=%async_computation.1 | async-start | bytes 1048576 | tf_op jit(solution)/shard_map/all_to_all | solution.py:72
  56.2 3.4 %copy-start.6 = (f32[512]{0:T(512)S(1)}, f32[512]{0:T(512)}, u32[]{:S(2)}) copy-start(f32[512]{0:T(512)} %param.18) | copy-start | bytes 6148
  59.4 8.0 %copy-start.1 = (bf16[4,4,2048]{2,1,0:T(4,128)(2,1)S(1)}, bf16[4,4,2048]{2,1,0:T(4,128)(2,1)}, u32[]{:S(2)}) copy-start(bf16[4,4,2048]{2,1,0:T(4,128)(2,1)} %param.10) | copy-start | bytes 196612
